TPU v7x, 256 devices: a whole 4x4x8 slice. The times are simulated.
256 devices in a mesh: req: 64 (over x, z, core), tp: 4 (over y).
Axes of the slice: x: 4, y: 4, z: 8, core: 2. Of those that a mesh axis runs over, the one named last changes fastest.
Arguments:
- hidden_in: bfloat16 [512, 1600], P('req'), may hold values from -6 to 6
- norm_gain: float32 [1600], replicated, may hold values from 0.1 to 1.9
- query_weight: bfloat16 [1600, 1280], P(None, 'tp'), may hold values from -0.15625 to 0.15625
- memory_weight: bfloat16 [1600, 512], P(None, 'tp'), may hold values from -0.15625 to 0.15625
- attention_out: bfloat16 [1280, 1600], P('tp'), may hold values from -0.15625 to 0.15625
- attention_gain: float32 [1280], P('tp'), may hold values from 0.1 to 1.9
- mamba_input: bfloat16 [2, 1600, 1600], P(None, None, 'tp'), may hold values from -0.15625 to 0.15625
- conv_weight: float32 [4, 1600], P(None, 'tp'), may hold values from -3 to 3
- conv_state: bfloat16 [512, 3, 1600], P('req', None, 'tp'), may hold values from -6 to 6
- select_weight: bfloat16 [1600, 132], P('tp'), may hold values from -0.15625 to 0.15625
- step_weight: bfloat16 [100, 1600], P(None, 'tp'), may hold values from -0.625 to 0.625
- step_bias: float32 [1600], P('tp'), may hold values from -4 to -1
- decay_log: float32 [16, 1600], P(None, 'tp'), may hold values from 0 to 2.77
- skip_gain: float32 [1600], P('tp'), may hold values from 0.5 to 1.5
- scan_state: float32 [512, 16, 1600], P('req', None, 'tp'), may hold values from -6 to 6
- mamba_gain: float32 [1600], P('tp'), may hold values from 0.1 to 1.9
- mamba_out: bfloat16 [1600, 1600], P('tp'), may hold values from -0.15625 to 0.15625
- cache_blocks: bfloat16 [2176, 4, 512, 128], P('req', 'tp'), as said below
- lengths: int32 [512], replicated, may hold values from 257 to 8192, as said below
- slot_request: int32 [2176], P('req'), may hold values from -1 to 511, as said below
- slot_block: int32 [2176], P('req'), may hold values from 0 to 15, as said below
Outputs:
- layer_out: bfloat16 [512, 1600], P('req', 'tp')
- new_state: float32 [512, 16, 1600], P('req', None, 'tp')
Inputs may be any that keep to these rules, and one draw needn't show every extreme that they name: `lengths`: some request holds exactly 8192 tokens. `slot_request`: -1 marks an empty slot; a request with L cached tokens fills exactly ceil(L / 512) slots; the slots of one index of req hold at most 2 blocks of the requests of any one index of req (requests r with equal r // 8), and some index of req holds exactly 2. `slot_block`: the slots of one request carry its block numbers 0 to ceil(L / 512) - 1, each once; empty slots carry 0. `cache_blocks`: the first 64 entries of the last dimension are keys, the rest values.
All inputs are finite; a program needn't handle non-finite values.
Results may differ from a plain program's by a relative error of at most 0.012.
Values may be sent and summed in bfloat16 or wider, within the bound.
A program may use at most 64 MiB of HBM per device.

v0:
```python
import jax
import jax.numpy as jnp
from jax import lax
from jax.sharding import PartitionSpec as P

HQ = 20
HD = 64
MI = 1600


def rotate_pairs(vector, position):
    head_dim = vector.shape[-1]
    half_dim = head_dim // 2
    frequency = jnp.power(
        jnp.float32(10000.0), -jnp.arange(half_dim, dtype=jnp.float32) * (2.0 / head_dim)
    )
    angles = position.astype(jnp.float32)[:, None, None] * frequency
    cosine = jnp.cos(angles)
    sine_part = jnp.sin(angles)
    front_half = vector[..., :half_dim]
    back_half = vector[..., half_dim:]
    return jnp.concatenate(
        [front_half * cosine - back_half * sine_part, back_half * cosine + front_half * sine_part],
        -1,
    )


def body(
    hidden_in,
    norm_gain,
    query_weight,
    memory_weight,
    attention_out,
    attention_gain,
    mamba_input,
    conv_weight,
    conv_state,
    select_weight,
    step_weight,
    step_bias,
    decay_log,
    skip_gain,
    scan_state,
    mamba_gain,
    mamba_out,
    cache_blocks,
    lengths,
    slot_request,
    slot_block,
):
    row_count = hidden_in.shape[0]
    model_width = hidden_in.shape[1]
    head_dim = cache_blocks.shape[3] // 2
    head_count = query_weight.shape[1] // head_dim
    block_len = cache_blocks.shape[2]
    slot_count = cache_blocks.shape[0]
    request_count = lengths.shape[0]
    holders = lax.axis_size("req")
    tp_count = lax.axis_size("tp")
    own_first = lax.axis_index("req") * row_count
    own_len = lax.dynamic_slice_in_dim(lengths, own_first, row_count)
    hidden_f = hidden_in.astype(jnp.float32)
    normed = (
        hidden_f * lax.rsqrt(jnp.mean(hidden_f * hidden_f, -1, keepdims=True) + 1e-06) * norm_gain
    ).astype(jnp.bfloat16)
    query_raw = jnp.dot(normed, query_weight, preferred_element_type=jnp.float32).reshape(
        row_count, head_count, head_dim
    )
    query = rotate_pairs(query_raw, own_len).astype(jnp.bfloat16)
    memory = jnp.dot(normed, memory_weight, preferred_element_type=jnp.float32)
    key_new = rotate_pairs(memory[:, None, :head_dim], own_len).astype(jnp.bfloat16)
    value_new = memory[:, head_dim:].astype(jnp.bfloat16)
    all_query = lax.all_gather(
        query.reshape(row_count, head_count * head_dim), "req", axis=0, tiled=True
    )
    slot_used = slot_request >= 0
    owner_row = jnp.where(slot_used, slot_request, 0)
    slot_query = jnp.take(all_query, owner_row, axis=0).reshape(slot_count, head_count, head_dim)
    keys = cache_blocks[:, 0, :, :head_dim]
    values = cache_blocks[:, 0, :, head_dim:]
    valid_len = jnp.where(slot_used, jnp.take(lengths, owner_row) - slot_block * block_len, 0)
    live_mask = jnp.arange(block_len)[None, :] < valid_len[:, None]
    scores = jnp.einsum(
        "shd,std->sht", slot_query, keys, preferred_element_type=jnp.float32
    ) * head_dim ** (-0.5)
    scores = jnp.where(live_mask[:, None, :], scores, -1e30)
    block_max = jnp.max(scores, 2)
    weights = jnp.where(live_mask[:, None, :], jnp.exp(scores - block_max[..., None]), 0.0).astype(
        jnp.bfloat16
    )
    block_sum = jnp.sum(weights.astype(jnp.float32), 2)
    block_out = jnp.einsum("sht,std->shd", weights, values, preferred_element_type=jnp.float32)
    own_score = jnp.sum(query.astype(jnp.float32) * key_new.astype(jnp.float32), -1) * head_dim ** (
        -0.5
    )
    value_own = value_new.astype(jnp.float32)[:, None, :]
    owner_match = slot_request[:, None] == jnp.arange(request_count)[None, :]
    request_max = jnp.max(jnp.where(owner_match[:, :, None], block_max[:, None, :], -1e30), axis=0)
    owner_table = owner_match.astype(jnp.float32)
    rescale = jnp.exp(block_max - jnp.take(request_max, owner_row, axis=0))
    scaled_out = (block_out * rescale[..., None]).reshape(slot_count, head_count * head_dim)
    part_out = jnp.dot(owner_table.T, scaled_out, precision=lax.Precision.HIGHEST)
    part_sum = jnp.dot(owner_table.T, block_sum * rescale, precision=lax.Precision.HIGHEST)
    part_out, part_sum = (part_out, part_sum)
    got_out, got_sum, got_max = (
        lax.all_to_all(
            part_out.reshape(holders, row_count, head_count * head_dim),
            "req",
            split_axis=0,
            concat_axis=0,
            tiled=True,
        ),
        lax.all_to_all(
            part_sum.reshape(holders, row_count, head_count),
            "req",
            split_axis=0,
            concat_axis=0,
            tiled=True,
        ),
        lax.all_to_all(
            request_max.reshape(holders, row_count, head_count),
            "req",
            split_axis=0,
            concat_axis=0,
            tiled=True,
        ),
    )
    top = jnp.maximum(jnp.max(got_max, 0), own_score)
    source_weight = jnp.exp(got_max - top[None])
    numer = jnp.sum(
        got_out.reshape(holders, row_count, head_count, head_dim) * source_weight[..., None], 0
    )
    denom = jnp.sum(got_sum * source_weight, 0)
    own_weight = jnp.exp(own_score - top)
    numer = numer + own_weight[..., None] * value_own
    denom = denom + own_weight
    attention = (numer / denom[..., None]).reshape(row_count, head_count * head_dim)
    mamba_x = jnp.dot(normed, mamba_input[0], preferred_element_type=jnp.float32).astype(
        jnp.bfloat16
    )
    gate_branch = jnp.dot(normed, mamba_input[1], preferred_element_type=jnp.float32)
    taps = conv_weight.shape[0]
    conv_sum = conv_weight[taps - 1] * mamba_x.astype(jnp.float32)
    for tap_index in range(taps - 1):
        conv_sum = conv_sum + conv_weight[tap_index] * conv_state[:, tap_index].astype(jnp.float32)
    activated = jax.nn.silu(conv_sum).astype(jnp.bfloat16)
    selection = lax.psum(
        jnp.dot(activated, select_weight, preferred_element_type=jnp.float32), "tp"
    )
    rank_width = step_weight.shape[0]
    state_width = decay_log.shape[0]
    step_rank = selection[:, :rank_width].astype(jnp.bfloat16)
    input_map = selection[:, rank_width : rank_width + state_width]
    output_map = selection[:, rank_width + state_width :]
    step_size = jax.nn.softplus(
        jnp.dot(step_rank, step_weight, preferred_element_type=jnp.float32) + step_bias
    )
    active_f = activated.astype(jnp.float32)
    new_state = (
        jnp.exp(-step_size[:, None, :] * jnp.exp(decay_log)[None]) * scan_state
        + step_size[:, None, :] * input_map[:, :, None] * active_f[:, None, :]
    )
    mamba_y = (jnp.sum(output_map[:, :, None] * new_state, 1) + skip_gain * active_f) * jax.nn.silu(
        gate_branch
    )
    attn_square = jnp.sum(attention * attention, -1)
    mamba_square = jnp.sum(mamba_y * mamba_y, -1)
    attn_used = (attention * attention_gain).astype(jnp.bfloat16)
    mamba_used = (mamba_y * mamba_gain).astype(jnp.bfloat16)
    attn_proj = jnp.dot(attn_used, attention_out, preferred_element_type=jnp.float32)
    mamba_proj = jnp.dot(mamba_used, mamba_out, preferred_element_type=jnp.float32)
    attn_total, mamba_total = lax.psum((attn_square, mamba_square), "tp")
    attn_scale = jnp.sqrt(attn_total / (HQ * HD) + 1e-06)
    mamba_scale = jnp.sqrt(mamba_total / MI + 1e-06)
    partial_value = 0.5 * (attn_proj / attn_scale[:, None] + mamba_proj / mamba_scale[:, None])
    mixed = lax.psum_scatter(partial_value, "tp", scatter_dimension=1, tiled=True)
    column_width = model_width // tp_count
    residual = lax.dynamic_slice_in_dim(
        hidden_f, lax.axis_index("tp") * column_width, column_width, 1
    )
    layer_out = (residual + mixed).astype(jnp.bfloat16)
    return (layer_out, new_state)


def solution(mesh):
    return jax.shard_map(
        body,
        mesh=mesh,
        in_specs=(
            P("req", None),
            P(),
            P(None, "tp"),
            P(None, "tp"),
            P("tp", None),
            P("tp"),
            P(None, None, "tp"),
            P(None, "tp"),
            P("req", None, "tp"),
            P("tp", None),
            P(None, "tp"),
            P("tp"),
            P(None, "tp"),
            P("tp"),
            P("req", None, "tp"),
            P("tp"),
            P("tp", None),
            P("req", "tp", None, None),
            P(),
            P("req"),
            P("req"),
        ),
        out_specs=(P("req", "tp"), P("req", None, "tp")),
        check_vma=False,
    )
```

profile of v0, /device:TPU:2, one launch (start us, length us, event | category | flops | bytes accessed | tf_op | source)
XLA Modules:
  0.0 191.9 jit_solution(11031688939695422736)
XLA Ops:
  7.2 0.8 compare_and_fusion
  8.0 0.7 iota_compare_fusion
  8.7 0.9 multiply_reduce_fusion.3
  9.6 1.3 fusion.74
  10.9 0.8 dynamic-slice_convert_fusion
  11.9 1.7 fusion.69
  14.0 50.3 %all_gather.3 = bf16[512,320]{1,0:T(8,128)(2,1)S(1)} all-gather(bf16[8,320]{1,0:T(8,128)(2,1)S(1)} %convert_element_type.89), channel_id=1, replica_groups=mesh['req'=64,'tp'=4] {'req'}, dimensions={0}, use_global_device_ids=true | all-gather | bytes 332800 | tf_op jit(solution)/shard_map/all_gather | solution.py:73
  64.3 0.8 gather_fusion
  65.1 0.6 gather_fusion.1
  66.0 3.6 %fusion.73 = (f32[34,5]{1,0:T(8,128)S(1)}, f32[34,5,512]{2,1,0:T(8,128)S(1)}) fusion(bf16[34,1,512,128]{3,2,1,0:T(8,128)(2,1)} %param.38, bf16[34,5,64]{2,1,0:T(8,128)(2,1)S(1)} %gather.16, pred[34]{0:T(512)(128)(4,1)S(1)} %get-tuple-element.14, pred[34,512]{1,0:T(8,128)(4,1)S(1)} %iota_compare_fusion.1), kind=kOutput, calls=%fused_computation.108 | convolution fusion | flops 11412950 | bytes 4844490 | tf_op jit(solution)/shard_map/shd,std->sht/dot_general | solution.py:83
  70.0 0.6 gather_fusion.2
  71.3 0.8 copy.72
  72.1 8.1 %all-to-all-start.2 = ((f32[64,8,5]{1,2,0:T(8,128)}), f32[64,8,5]{1,2,0:T(8,128)S(1)}, u32[]{:S(2)}, u32[]{:S(2)}) async-start(f32[64,8,5]{1,2,0:T(8,128)} %copy.72), calls=%async_computation.2 | async-start | bytes 524288 | tf_op jit(solution)/shard_map/all_to_all | solution.py:113
  80.3 3.7 %fusion.20 = f32[34,5,64]{2,1,0:T(8,128)S(1)} fusion(bf16[34,1,512,128]{3,2,1,0:T(8,128)(2,1)} %param.38, f32[34,5]{1,0:T(8,128)S(1)} %subtract_exponential_fusion.1, f32[34,5,512]{2,1,0:T(8,128)S(1)} %get-tuple-element.29, f32[34,5]{1,0:T(8,128)S(1)} %get-tuple-element.28, pred[34,512]{1,0:T(8,128)(4,1)S(1)} %iota_compare_fusion.1), kind=kOutput, calls=%fused_computation.21 | convolution fusion | flops 11413120 | bytes 4866896 | tf_op jit(solution)/shard_map/sht,std->shd/dot_general | solution.py:92
  84.2 1.8 fusion.75
  86.2 10.8 %psum.22 = f32[8,132]{1,0:T(8,128)S(1)} all-reduce(f32[8,132]{1,0:T(8,128)S(1)} %fusion.77), channel_id=1, replica_groups=mesh['req'=64,'tp'=4] {'tp'}, use_global_device_ids=true, to_apply=%region_10.11 | all-reduce | flops 1056 | bytes 8448 | tf_op jit(solution)/shard_map/psum | solution.py:147
  97.1 1.4 fusion.41
  98.8 0.8 copy.67
  99.7 10.3 %all-to-all-start.1 = ((f32[64,8,5]{1,2,0:T(8,128)}), f32[64,8,5]{1,2,0:T(8,128)S(1)}, u32[]{:S(2)}, u32[]{:S(2)}) async-start(f32[64,8,5]{1,2,0:T(8,128)} %copy.67), calls=%async_computation.1 | async-start | bytes 524288 | tf_op jit(solution)/shard_map/all_to_all | solution.py:120
  110.0 0.9 multiply_reduce_fusion.1
  110.9 10.7 %all-to-all-done.1 = f32[64,8,5]{1,2,0:T(8,128)S(1)} async-done(((f32[64,8,5]{1,2,0:T(8,128)}), f32[64,8,5]{1,2,0:T(8,128)S(1)}, u32[]{:S(2)}, u32[]{:S(2)}) %all-to-all-start.1) | async-done | bytes 10272 | tf_op jit(solution)/shard_map/all_to_all | solution.py:120
  121.6 6.5 %all-to-all-start = ((f32[64,8,320]{2,1,0:T(8,128)}), f32[64,8,320]{2,1,0:T(8,128)S(1)}, u32[]{:S(2)}, u32[]{:S(2)}) async-start(f32[64,8,320]{2,1,0:T(8,128)} %fusion.41), calls=%async_computation | async-start | bytes 1572864 | tf_op jit(solution)/shard_map/all_to_all | solution.py:106
  128.3 1.9 %multiply_reduce_fusion.5 = (f32[8]{0:T(128)S(1)}, f32[8,400]{1,0:T(8,128)S(1)}) fusion(bf16[2,1600,400]{1,2,0:T(8,128)(2,1)} %param.27, f32[1600]{0:T(1024)S(1)} %copy-done.7, f32[8]{0:T(128)S(1)} %add_rsqrt_fusion, bf16[8,1600]{1,0:T(8,128)(2,1)S(1)} %copy-done.3, f32[8,400]{1,0:T(8,128)S(1)} %get-tuple-element.4, ...), kind=kOutput, calls=%fused_computation.61 | convolution fusion | flops 10323192 | bytes 1396864 | tf_op jit(solution)/shard_map/dot_general | solution.py:141
  130.6 1.4 copy.70
  132.5 17.5 %all-to-all-done = f32[64,8,320]{2,1,0:T(8,128)S(1)} async-done(((f32[64,8,320]{2,1,0:T(8,128)}), f32[64,8,320]{2,1,0:T(8,128)S(1)}, u32[]{:S(2)}, u32[]{:S(2)}) %all-to-all-start) | async-done | bytes 655392 | tf_op jit(solution)/shard_map/all_to_all | solution.py:106
  149.9 1.3 multiply_reduce_fusion
  151.4 7.7 %all-reduce = (f32[8]{0:T(128)S(1)}, f32[8]{0:T(128)S(1)}) all-reduce(f32[8]{0:T(128)S(1)} %get-tuple-element.6, f32[8]{0:T(128)S(1)} %get-tuple-element.36), channel_id=1, replica_groups=mesh['req'=64,'tp'=4] {'tp'}, use_global_device_ids=true, to_apply=%region_9.10 | all-reduce | flops 16 | bytes 128 | tf_op jit(solution)/shard_map/psum | solution.py:172
  159.4 0.3 fusion.7
  159.7 1.2 copy.74
  160.9 22.4 %reduce-scatter.4.cloned.1.call-done = f32[400,8]{1,0:T(8,128)} async-done(((f32[1600,8]{1,0:T(8,128)}), f32[400,8]{1,0:T(8,128)}) %reduce-scatter.4.cloned.1.call-update) | async-done | bytes 12816
  183.3 1.0 copy.75
  184.3 0.7 add_convert_fusion
  (82 shorter events, 4.2 us)
Async XLA Ops:
  7.2 152.2 %copy-start = (bf16[400,1600]{1,0:T(8,128)(2,1)S(1)}, bf16[400,1600]{1,0:T(8,128)(2,1)}, u32[]{:S(2)}) copy-start(bf16[400,1600]{1,0:T(8,128)(2,1)} %param.37) | copy-start | bytes 3840004
  7.2 57.2 %copy-start.1 = (s32[512]{0:T(512)S(1)}, s32[512]{0:T(512)}, u32[]{:S(2)}) copy-start(s32[512]{0:T(512)} %param.39) | copy-start | bytes 6148
  11.9 54.0 %copy-start.10 = (s32[34]{0:T(128)S(1)}, s32[34]{0:T(128)}, u32[]{:S(2)}) copy-start(s32[34]{0:T(128)} %param.40) | copy-start | bytes 412
  11.9 54.0 %copy-start.14 = (s32[34]{0:T(128)S(1)}, s32[34]{0:T(128)}, u32[]{:S(2)}) copy-start(s32[34]{0:T(128)} %param.41) | copy-start | bytes 412
  72.1 27.5 %all-to-all-start.2 = ((f32[64,8,5]{1,2,0:T(8,128)}), f32[64,8,5]{1,2,0:T(8,128)S(1)}, u32[]{:S(2)}, u32[]{:S(2)}) async-start(f32[64,8,5]{1,2,0:T(8,128)} %copy.72), calls=%async_computation.2 | async-start | bytes 524288 | tf_op jit(solution)/shard_map/all_to_all | solution.py:113
  80.2 3.9 %copy-start.9 = (f32[4,400]{1,0:T(4,128)S(1)}, f32[4,400]{1,0:T(4,128)}, u32[]{:S(2)}) copy-start(f32[4,400]{1,0:T(4,128)} %param.28) | copy-start | bytes 19204
  80.3 3.9 %copy-start.3 = (bf16[8,1600]{1,0:T(8,128)(2,1)S(1)}, bf16[8,1600]{1,0:T(8,128)(2,1)}, u32[]{:S(2)}) copy-start(bf16[8,1600]{1,0:T(8,128)(2,1)} %param.21) | copy-start | bytes 76804
  80.3 3.9 %copy-start.7 = (f32[1600]{0:T(1024)S(1)}, f32[1600]{0:T(1024)}, u32[]{:S(2)}) copy-start(f32[1600]{0:T(1024)} %param.22) | copy-start | bytes 19204
  84.0 2.1 %copy-start.5 = (bf16[400,132]{0,1:T(8,128)(2,1)S(1)}, bf16[400,132]{0,1:T(8,128)(2,1)}, u32[]{:S(2)}) copy-start(bf16[400,132]{0,1:T(8,128)(2,1)} %param.30) | copy-start | bytes 316804
  84.1 14.3 %copy-start.6 = (bf16[100,400]{0,1:T(8,128)(2,1)S(1)}, bf16[100,400]{0,1:T(8,128)(2,1)}, u32[]{:S(2)}) copy-start(bf16[100,400]{0,1:T(8,128)(2,1)} %param.31) | copy-start | bytes 240004
  84.1 14.3 %copy-start.11 = (f32[400]{0:T(512)S(1)}, f32[400]{0:T(512)}, u32[]{:S(2)}) copy-start(f32[400]{0:T(512)} %param.32) | copy-start | bytes 4804
  84.2 15.5 %copy-start.8 = (f32[16,400]{1,0:T(8,128)S(1)}, f32[16,400]{1,0:T(8,128)}, u32[]{:S(2)}) copy-start(f32[16,400]{1,0:T(8,128)} %param.33) | copy-start | bytes 76804
  86.1 24.0 %copy-start.4 = (f32[8,16,400]{2,1,0:T(8,128)S(1)}, f32[8,16,400]{2,1,0:T(8,128)}, u32[]{:S(2)}) copy-start(f32[8,16,400]{2,1,0:T(8,128)} %param.35) | copy-start | bytes 614404
  99.7 28.6 %copy-start.15 = (f32[400]{0:T(512)S(1)}, f32[400]{0:T(512)}, u32[]{:S(2)}) copy-start(f32[400]{0:T(512)} %param.34) | copy-start | bytes 4804
  99.7 21.9 %all-to-all-start.1 = ((f32[64,8,5]{1,2,0:T(8,128)}), f32[64,8,5]{1,2,0:T(8,128)S(1)}, u32[]{:S(2)}, u32[]{:S(2)}) async-start(f32[64,8,5]{1,2,0:T(8,128)} %copy.67), calls=%async_computation.1 | async-start | bytes 524288 | tf_op jit(solution)/shard_map/all_to_all | solution.py:120
  121.6 28.4 %all-to-all-start = ((f32[64,8,320]{2,1,0:T(8,128)}), f32[64,8,320]{2,1,0:T(8,128)S(1)}, u32[]{:S(2)}, u32[]{:S(2)}) async-start(f32[64,8,320]{2,1,0:T(8,128)} %fusion.41), calls=%async_computation | async-start | bytes 1572864 | tf_op jit(solution)/shard_map/all_to_all | solution.py:106
  128.1 55.2 %reduce-scatter.4.cloned.1.call-start = ((), (), s32[]{:S(2)}) async-start(), calls=%async_computation.4 | async-start | bytes 1024000
  132.0 27.1 %copy-start.2 = (bf16[320,1600]{1,0:T(8,128)(2,1)S(1)}, bf16[320,1600]{1,0:T(8,128)(2,1)}, u32[]{:S(2)}) copy-start(bf16[320,1600]{1,0:T(8,128)(2,1)} %param.25) | copy-start | bytes 3072004
  132.0 27.1 %copy-start.12 = (f32[320]{0:T(512)S(1)}, f32[320]{0:T(512)}, u32[]{:S(2)}) copy-start(f32[320]{0:T(512)} %param.26) | copy-start | bytes 3844
  132.5 26.9 %copy-start.13 = (f32[400]{0:T(512)S(1)}, f32[400]{0:T(512)}, u32[]{:S(2)}) copy-start(f32[400]{0:T(512)} %param.36) | copy-start | bytes 4804
Sparse Core Ops, SparseCore 0:
  161.0 22.2 reduce-scatter.3
where the time goes:
time: 193 us; the launch traced here: 192 us
  blocking collectives  68.9 us (36%)
  waiting for transfers between devices  50.5 us (26%)
  starting transfers between devices  25 us (13%)
  matrix products  16.5 us (9%)
  between operations  14.4 us (7%)
  local copies, waits for them, and re-layouts  8.94 us (5%)
  other arithmetic  7.63 us (4%)
    all_gather x1, blocking collectives, body(): lax.all_gather(query.reshape(row_count, head_count * head_dim), 'req', ax...  50.3 us
    unnamed x2, waiting for transfers between devices  22.4 us
    all_to_all x1, waiting for transfers between devices, body(): lax.all_to_all(part_out.reshape(holders, row_count, head_count * head_dim...  17.5 us
    psum x1, blocking collectives, body(): lax.psum(jnp.dot(activated, select_weight, preferred_element_type=jnp.flo...  10.8 us
    all_to_all x1, waiting for transfers between devices, body(): lax.all_to_all(request_max.reshape(holders, row_count, head_count), 'req'...  10.7 us
    all_to_all x1, starting transfers between devices, body(): lax.all_to_all(request_max.reshape(holders, row_count, head_count), 'req'...  10.3 us
    all_to_all x1, starting transfers between devices, body(): lax.all_to_all(part_sum.reshape(holders, row_count, head_count), 'req', s...  8.09 us
    psum x1, blocking collectives, body(): attn_total, mamba_total = lax.psum((attn_square, mamba_square), 'tp')  7.74 us
  transfers between devices with their start and end apart: 4, of which 3 were waited for; matrix products, arithmetic and copies ran while one was open for 7% of the time, Pallas kernels for 0%

commit v1 on v0

--- a/solution.py
+++ b/solution.py
@@ -70,8 +70,14 @@
     memory = jnp.dot(normed, memory_weight, preferred_element_type=jnp.float32)
     key_new = rotate_pairs(memory[:, None, :head_dim], own_len).astype(jnp.bfloat16)
     value_new = memory[:, head_dim:].astype(jnp.bfloat16)
-    all_query = lax.all_gather(
-        query.reshape(row_count, head_count * head_dim), "req", axis=0, tiled=True
+    all_query = jnp.concatenate(
+        lax.all_to_all(
+            jnp.stack([query.reshape(row_count, head_count * head_dim)] * lax.axis_size("req")),
+            "req",
+            0,
+            0,
+        ),
+        axis=0,
     )
     slot_used = slot_request >= 0
     owner_row = jnp.where(slot_used, slot_request, 0)

time: 193 us -> 159 us (0.82)
  blocking collectives: 68.9 us -> 18.6 us
  starting transfers between devices: 25 us -> 35.5 us
  waiting for transfers between devices: 50.5 us -> 56.8 us
    all_gather x1 -> x0, blocking collectives: 50.3 us -> none  [body(): lax.all_gather(query.reshape(row_count, head_count * head_dim), 'req', ax...]
    all_to_all x0 -> x1, starting transfers between devices: none -> 12.2 us  [body(): lax.all_to_all(jnp.stack([query.reshape(row_count, head_count * head_dim)...]
    all_to_all x1, waiting for transfers between devices: 0.01 us -> 6.8 us  [body(): lax.all_to_all(part_sum.reshape(holders, row_count, head_count), 'req', s...]
    all_to_all x1, starting transfers between devices: 10.3 us -> 6.49 us  [body(): lax.all_to_all(request_max.reshape(holders, row_count, head_count), 'req'...]
    all_to_all x1, starting transfers between devices: 8.09 us -> 10.3 us  [body(): lax.all_to_all(part_sum.reshape(holders, row_count, head_count), 'req', s...]
  transfers between devices with their start and end apart: 4 -> 5, of which waited for: 3 -> 4; matrix products, arithmetic and copies ran while one was open for 7% -> 9% of each run, Pallas kernels for 0% -> 0%
where the time goes in v1:
time: 159 us; the launch traced here: 158 us
  waiting for transfers between devices  56.8 us (36%)
  starting transfers between devices  35.5 us (22%)
  blocking collectives  18.6 us (12%)
  matrix products  16.5 us (10%)
  between operations  14.4 us (9%)
  local copies, waits for them, and re-layouts  9.73 us (6%)
  other arithmetic  6.36 us (4%)
    unnamed x2, waiting for transfers between devices  22.4 us
    all_to_all x1, waiting for transfers between devices, body(): lax.all_to_all(part_out.reshape(holders, row_count, head_count * head_dim...  17.5 us
    all_to_all x1, starting transfers between devices, body(): lax.all_to_all(jnp.stack([query.reshape(row_count, head_count * head_dim)...  12.2 us
    psum x1, blocking collectives, body(): lax.psum(jnp.dot(activated, select_weight, preferred_element_type=jnp.flo...  10.8 us
    all_to_all x1, starting transfers between devices, body(): lax.all_to_all(part_sum.reshape(holders, row_count, head_count), 'req', s...  10.3 us
    all_to_all x1, waiting for transfers between devices, body(): lax.all_to_all(request_max.reshape(holders, row_count, head_count), 'req'...  10.1 us
    psum x1, blocking collectives, body(): attn_total, mamba_total = lax.psum((attn_square, mamba_square), 'tp')  7.74 us
    all_to_all x1, waiting for transfers between devices, body(): lax.all_to_all(part_sum.reshape(holders, row_count, head_count), 'req', s...  6.8 us
  transfers between devices with their start and end apart: 5, of which 4 were waited for; matrix products, arithmetic and copies ran while one was open for 9% of the time, Pallas kernels for 0%

profile of v1, /device:TPU:2, one launch (start us, length us, event | category | flops | bytes accessed | tf_op | source)
XLA Modules:
  0.0 157.9 jit_solution(17377567592609342714)
XLA Ops:
  7.2 1.0 multiply_reduce_fusion.3
  8.2 1.3 fusion.74
  9.5 0.8 dynamic-slice_convert_fusion
  10.6 1.7 %fusion.69 = f32[8,320]{1,0:T(8,128)S(1)} fusion(bf16[1600,320]{0,1:T(8,128)(2,1)} %param.23, f32[1600]{0:T(1024)} %param.22, f32[8]{0:T(128)S(1)} %add_rsqrt_fusion, bf16[8,1600]{1,0:T(8,128)(2,1)} %param.21), kind=kOutput, calls=%fused_computation.104 | convolution fusion | flops 8243200 | bytes 1066272 | tf_op jit(solution)/shard_map/dot_general | solution.py:66
  12.7 0.8 stack.3
  13.5 12.2 %all-to-all-start = ((bf16[64,8,320]{2,1,0:T(8,128)(2,1)}), bf16[64,8,320]{2,1,0:T(8,128)(2,1)S(1)}, u32[]{:S(2)}, u32[]{:S(2)}) async-start(bf16[64,8,320]{2,1,0:T(8,128)(2,1)} %stack.3), calls=%async_computation | async-start | bytes 786432 | tf_op jit(solution)/shard_map/all_to_all | solution.py:74
  25.9 0.8 gather_fusion
  26.8 1.8 %fusion.75 = (f32[8,400]{1,0:T(8,128)S(1)}, bf16[8,400]{1,0:T(8,128)(2,1)S(1)}) fusion(bf16[8,3,400]{2,0,1:T(8,128)(2,1)} %param.29, f32[400]{0:T(512)S(1)} %bitcast.83, f32[400]{0:T(512)S(1)} %bitcast.84, f32[400]{0:T(512)S(1)} %bitcast.82, bf16[2,1600,400]{1,2,0:T(8,128)(2,1)} %param.27, f32[1600]{0:T(1024)S(1)} %copy-done.7, f32[8]{0:T(128)S(1)} %add_rsqrt_fusion, ...), kind=kOutput, calls=%fused_computation.110 | convolution fusion | flops 10348800 | bytes 1413408 | tf_op jit(solution)/shard_map/dot_general | solution.py:144
  28.8 10.8 %psum.22 = f32[8,132]{1,0:T(8,128)S(1)} all-reduce(f32[8,132]{1,0:T(8,128)S(1)} %fusion.77), channel_id=1, replica_groups=mesh['req'=64,'tp'=4] {'tp'}, use_global_device_ids=true, to_apply=%region_10.11 | all-reduce | flops 1056 | bytes 8448 | tf_op jit(solution)/shard_map/psum | solution.py:153
  40.0 0.9 multiply_reduce_fusion.1
  40.8 0.6 gather_fusion.1
  41.6 3.6 %fusion.73 = (f32[34,5]{1,0:T(8,128)S(1)}, f32[34,5,512]{2,1,0:T(8,128)S(1)}) fusion(bf16[34,1,512,128]{3,2,1,0:T(8,128)(2,1)} %param.38, bf16[34,5,64]{2,1,0:T(8,128)(2,1)S(1)} %gather.16, pred[34]{0:T(512)(128)(4,1)S(1)} %get-tuple-element.14, pred[34,512]{1,0:T(8,128)(4,1)S(1)} %iota_compare_fusion.1), kind=kOutput, calls=%fused_computation.108 | convolution fusion | flops 11412950 | bytes 4844490 | tf_op jit(solution)/shard_map/shd,std->sht/dot_general | solution.py:89
  45.6 0.6 gather_fusion.2
  46.9 0.8 copy.72
  47.7 10.3 %all-to-all-start.3 = ((f32[64,8,5]{1,2,0:T(8,128)}), f32[64,8,5]{1,2,0:T(8,128)S(1)}, u32[]{:S(2)}, u32[]{:S(2)}) async-start(f32[64,8,5]{1,2,0:T(8,128)} %copy.72), calls=%async_computation.3 | async-start | bytes 524288 | tf_op jit(solution)/shard_map/all_to_all | solution.py:119
  58.1 3.7 %fusion.20 = f32[34,5,64]{2,1,0:T(8,128)S(1)} fusion(bf16[34,1,512,128]{3,2,1,0:T(8,128)(2,1)} %param.38, f32[34,5]{1,0:T(8,128)S(1)} %subtract_exponential_fusion.1, f32[34,5,512]{2,1,0:T(8,128)S(1)} %get-tuple-element.29, f32[34,5]{1,0:T(8,128)S(1)} %get-tuple-element.28, pred[34,512]{1,0:T(8,128)(4,1)S(1)} %iota_compare_fusion.1), kind=kOutput, calls=%fused_computation.21 | convolution fusion | flops 11413120 | bytes 4866896 | tf_op jit(solution)/shard_map/sht,std->shd/dot_general | solution.py:98
  61.9 0.8 copy.67
  62.8 6.8 %all-to-all-done.3 = f32[64,8,5]{1,2,0:T(8,128)S(1)} async-done(((f32[64,8,5]{1,2,0:T(8,128)}), f32[64,8,5]{1,2,0:T(8,128)S(1)}, u32[]{:S(2)}, u32[]{:S(2)}) %all-to-all-start.3) | async-done | bytes 10272 | tf_op jit(solution)/shard_map/all_to_all | solution.py:119
  69.6 6.5 %all-to-all-start.2 = ((f32[64,8,5]{1,2,0:T(8,128)}), f32[64,8,5]{1,2,0:T(8,128)S(1)}, u32[]{:S(2)}, u32[]{:S(2)}) async-start(f32[64,8,5]{1,2,0:T(8,128)} %copy.67), calls=%async_computation.2 | async-start | bytes 524288 | tf_op jit(solution)/shard_map/all_to_all | solution.py:126
  76.1 1.4 fusion.41
  77.5 10.1 %all-to-all-done.2 = f32[64,8,5]{1,2,0:T(8,128)S(1)} async-done(((f32[64,8,5]{1,2,0:T(8,128)}), f32[64,8,5]{1,2,0:T(8,128)S(1)}, u32[]{:S(2)}, u32[]{:S(2)}) %all-to-all-start.2) | async-done | bytes 10272 | tf_op jit(solution)/shard_map/all_to_all | solution.py:126
  87.6 6.5 %all-to-all-start.1 = ((f32[64,8,320]{2,1,0:T(8,128)}), f32[64,8,320]{2,1,0:T(8,128)S(1)}, u32[]{:S(2)}, u32[]{:S(2)}) async-start(f32[64,8,320]{2,1,0:T(8,128)} %fusion.41), calls=%async_computation.1 | async-start | bytes 1572864 | tf_op jit(solution)/shard_map/all_to_all | solution.py:112
  94.3 1.9 %multiply_reduce_fusion.5 = (f32[8]{0:T(128)S(1)}, f32[8,400]{1,0:T(8,128)S(1)}) fusion(bf16[2,1600,400]{1,2,0:T(8,128)(2,1)} %param.27, f32[1600]{0:T(1024)S(1)} %copy-done.7, f32[8]{0:T(128)S(1)} %add_rsqrt_fusion, bf16[8,1600]{1,0:T(8,128)(2,1)S(1)} %copy-done.3, f32[8,400]{1,0:T(8,128)S(1)} %get-tuple-element.4, ...), kind=kOutput, calls=%fused_computation.61 | convolution fusion | flops 10323192 | bytes 1396864 | tf_op jit(solution)/shard_map/dot_general | solution.py:147
  96.7 1.4 copy.70
  98.5 17.5 %all-to-all-done.1 = f32[64,8,320]{2,1,0:T(8,128)S(1)} async-done(((f32[64,8,320]{2,1,0:T(8,128)}), f32[64,8,320]{2,1,0:T(8,128)S(1)}, u32[]{:S(2)}, u32[]{:S(2)}) %all-to-all-start.1) | async-done | bytes 655392 | tf_op jit(solution)/shard_map/all_to_all | solution.py:112
  116.0 1.3 multiply_reduce_fusion
  117.4 7.7 %all-reduce = (f32[8]{0:T(128)S(1)}, f32[8]{0:T(128)S(1)}) all-reduce(f32[8]{0:T(128)S(1)} %get-tuple-element.6, f32[8]{0:T(128)S(1)} %get-tuple-element.36), channel_id=1, replica_groups=mesh['req'=64,'tp'=4] {'tp'}, use_global_device_ids=true, to_apply=%region_9.10 | all-reduce | flops 16 | bytes 128 | tf_op jit(solution)/shard_map/psum | solution.py:178
  125.5 0.3 fusion.7
  125.7 1.2 copy.74
  127.0 22.4 %reduce-scatter.4.cloned.1.call-done = f32[400,8]{1,0:T(8,128)} async-done(((f32[1600,8]{1,0:T(8,128)}), f32[400,8]{1,0:T(8,128)}) %reduce-scatter.4.cloned.1.call-update) | async-done | bytes 12816
  149.4 1.0 copy.75
  150.4 0.7 add_convert_fusion
  (84 shorter events, 4.3 us)
Async XLA Ops:
  7.2 118.3 %copy-start = (bf16[400,1600]{1,0:T(8,128)(2,1)S(1)}, bf16[400,1600]{1,0:T(8,128)(2,1)}, u32[]{:S(2)}) copy-start(bf16[400,1600]{1,0:T(8,128)(2,1)} %param.37) | copy-start | bytes 3840004
  9.4 16.3 %copy-start.10 = (s32[34]{0:T(128)S(1)}, s32[34]{0:T(128)}, u32[]{:S(2)}) copy-start(s32[34]{0:T(128)} %param.40) | copy-start | bytes 412
  9.4 16.4 %copy-start.1 = (s32[512]{0:T(512)S(1)}, s32[512]{0:T(512)}, u32[]{:S(2)}) copy-start(s32[512]{0:T(512)} %param.39) | copy-start | bytes 6148
  10.5 16.2 %copy-start.14 = (s32[34]{0:T(128)S(1)}, s32[34]{0:T(128)}, u32[]{:S(2)}) copy-start(s32[34]{0:T(128)} %param.41) | copy-start | bytes 412
  10.5 16.3 %copy-start.9 = (f32[4,400]{1,0:T(4,128)S(1)}, f32[4,400]{1,0:T(4,128)}, u32[]{:S(2)}) copy-start(f32[4,400]{1,0:T(4,128)} %param.28) | copy-start | bytes 19204
  10.5 16.3 %copy-start.3 = (bf16[8,1600]{1,0:T(8,128)(2,1)S(1)}, bf16[8,1600]{1,0:T(8,128)(2,1)}, u32[]{:S(2)}) copy-start(bf16[8,1600]{1,0:T(8,128)(2,1)} %param.21) | copy-start | bytes 76804
  10.5 16.3 %copy-start.7 = (f32[1600]{0:T(1024)S(1)}, f32[1600]{0:T(1024)}, u32[]{:S(2)}) copy-start(f32[1600]{0:T(1024)} %param.22) | copy-start | bytes 19204
  13.5 15.2 %copy-start.5 = (bf16[400,132]{0,1:T(8,128)(2,1)S(1)}, bf16[400,132]{0,1:T(8,128)(2,1)}, u32[]{:S(2)}) copy-start(bf16[400,132]{0,1:T(8,128)(2,1)} %param.30) | copy-start | bytes 316804
  13.5 27.3 %all-to-all-start = ((bf16[64,8,320]{2,1,0:T(8,128)(2,1)}), bf16[64,8,320]{2,1,0:T(8,128)(2,1)S(1)}, u32[]{:S(2)}, u32[]{:S(2)}) async-start(bf16[64,8,320]{2,1,0:T(8,128)(2,1)} %stack.3), calls=%async_computation | async-start | bytes 786432 | tf_op jit(solution)/shard_map/all_to_all | solution.py:74
  25.7 14.0 %copy-start.8 = (f32[16,400]{1,0:T(8,128)S(1)}, f32[16,400]{1,0:T(8,128)}, u32[]{:S(2)}) copy-start(f32[16,400]{1,0:T(8,128)} %param.33) | copy-start | bytes 76804
  25.7 14.1 %copy-start.6 = (bf16[100,400]{0,1:T(8,128)(2,1)S(1)}, bf16[100,400]{0,1:T(8,128)(2,1)}, u32[]{:S(2)}) copy-start(bf16[100,400]{0,1:T(8,128)(2,1)} %param.31) | copy-start | bytes 240004
  25.7 14.1 %copy-start.11 = (f32[400]{0:T(512)S(1)}, f32[400]{0:T(512)}, u32[]{:S(2)}) copy-start(f32[400]{0:T(512)} %param.32) | copy-start | bytes 4804
  25.7 14.2 %copy-start.4 = (f32[8,16,400]{2,1,0:T(8,128)S(1)}, f32[8,16,400]{2,1,0:T(8,128)}, u32[]{:S(2)}) copy-start(f32[8,16,400]{2,1,0:T(8,128)} %param.35) | copy-start | bytes 614404
  47.7 21.9 %all-to-all-start.3 = ((f32[64,8,5]{1,2,0:T(8,128)}), f32[64,8,5]{1,2,0:T(8,128)S(1)}, u32[]{:S(2)}, u32[]{:S(2)}) async-start(f32[64,8,5]{1,2,0:T(8,128)} %copy.72), calls=%async_computation.3 | async-start | bytes 524288 | tf_op jit(solution)/shard_map/all_to_all | solution.py:119
  69.6 18.0 %all-to-all-start.2 = ((f32[64,8,5]{1,2,0:T(8,128)}), f32[64,8,5]{1,2,0:T(8,128)S(1)}, u32[]{:S(2)}, u32[]{:S(2)}) async-start(f32[64,8,5]{1,2,0:T(8,128)} %copy.67), calls=%async_computation.2 | async-start | bytes 524288 | tf_op jit(solution)/shard_map/all_to_all | solution.py:126
  76.1 18.2 %copy-start.15 = (f32[400]{0:T(512)S(1)}, f32[400]{0:T(512)}, u32[]{:S(2)}) copy-start(f32[400]{0:T(512)} %param.34) | copy-start | bytes 4804
  87.6 28.4 %all-to-all-start.1 = ((f32[64,8,320]{2,1,0:T(8,128)}), f32[64,8,320]{2,1,0:T(8,128)S(1)}, u32[]{:S(2)}, u32[]{:S(2)}) async-start(f32[64,8,320]{2,1,0:T(8,128)} %fusion.41), calls=%async_computation.1 | async-start | bytes 1572864 | tf_op jit(solution)/shard_map/all_to_all | solution.py:112
  94.1 55.2 %reduce-scatter.4.cloned.1.call-start = ((), (), s32[]{:S(2)}) async-start(), calls=%async_computation.5 | async-start | bytes 1024000
  98.0 27.1 %copy-start.2 = (bf16[320,1600]{1,0:T(8,128)(2,1)S(1)}, bf16[320,1600]{1,0:T(8,128)(2,1)}, u32[]{:S(2)}) copy-start(bf16[320,1600]{1,0:T(8,128)(2,1)} %param.25) | copy-start | bytes 3072004
  98.0 27.1 %copy-start.12 = (f32[320]{0:T(512)S(1)}, f32[320]{0:T(512)}, u32[]{:S(2)}) copy-start(f32[320]{0:T(512)} %param.26) | copy-start | bytes 3844
  98.5 26.9 %copy-start.13 = (f32[400]{0:T(512)S(1)}, f32[400]{0:T(512)}, u32[]{:S(2)}) copy-start(f32[400]{0:T(512)} %param.36) | copy-start | bytes 4804
Sparse Core Ops, SparseCore 0:
  127.1 22.2 reduce-scatter.3
